TPU v7x, 128 devices: a whole 4x4x4 slice. The times are simulated.
128 devices in a mesh: basis: 4 (over z), pair: 32 (over x, y, core).
Axes of the slice: x: 4, y: 4, z: 4, core: 2. Of those that a mesh axis runs over, the one named last changes fastest.
Arguments:
- half_ints: bfloat16 [64, 16384, 256], P('pair', 'basis'), may hold values from -6 to 6
- pno_coef: bfloat16 [4, 128, 16384, 128], P(None, 'pair', 'basis'), may hold values from -0.046875 to 0.046875
- pair_list: int32 [4, 128, 2], P(None, 'pair'), may hold values from 0 to 63, as said below
- fit_domain: int32 [64, 256], P('pair'), may hold values from 0 to 32767
- fit_factor: bfloat16 [32768, 256], P('pair'), may hold values from -0.375 to 0.375
- amplitudes: bfloat16 [512, 128, 128], P(('basis', 'pair')), may hold values from -3 to 3
- pno_energy: float32 [512, 128], P(('basis', 'pair')), may hold values from 0.3 to 3
- occ_energy: float32 [64], replicated, may hold values from -2 to -0.3
- partners: int32 [512, 8], P(('basis', 'pair')), may hold values from 0 to 511, as said below
- partner_mask: int32 [512, 8], P(('basis', 'pair')), may hold values from 0 to 1, as said below
- intersections: bfloat16 [512, 8, 128, 128], P(('basis', 'pair')), may hold values from -0.5 to 0.5
- coupling: float32 [512, 8], P(('basis', 'pair')), may hold values from -3 to 3
Outputs:
- residual: float32 [512, 128, 128], P(('basis', 'pair'))
- new_amplitudes: bfloat16 [512, 128, 128], P(('basis', 'pair'))
Inputs may be any that keep to these rules, and one draw needn't show every extreme that they name: pair_list[b, h, 0] lies in (h // 4) * 2 to (h // 4 + 1) * 2 - 1. `partners`: every partner of pair b * 128 + h lies in b * 128 to (b + 1) * 128 - 1; among the 32 slots of the pairs of one device, at most 2 name pairs of one device, and exactly 2 do for some device. `partner_mask`: the valid slots of each pair come first, and the first slot is valid.
All inputs are finite; a program needn't handle non-finite values.
Results may differ from a plain program's by a relative error of at most 0.008.
Values may be sent and summed in bfloat16 or wider, within the bound.
A program may use at most 128 MiB of HBM per device.

v0:
```python
import jax
import jax.numpy as jnp
from jax import lax
from jax.sharding import PartitionSpec as P


def pick_rows(table, index):
    return lax.dynamic_index_in_dim(table, index, 0, keepdims=False)


def take_inside(wanted_index, shard_rows):
    inside = (wanted_index >= 0) & (wanted_index < shard_rows.shape[0])
    safe_index = jnp.clip(wanted_index, 0, shard_rows.shape[0] - 1)
    taken = jnp.take(shard_rows, safe_index, axis=0).astype(jnp.float32)
    return jnp.where(inside[:, None], taken, 0.0)


def shards(
    half_ints,
    pno_coef,
    pair_list,
    fit_domain,
    fit_factor,
    amplitudes,
    pno_energy,
    occ_energy,
    partners,
    partner_mask,
    intersections,
    coupling,
):
    pair_count = lax.axis_size("pair")
    my_basis = lax.axis_index("basis")
    my_pair = lax.axis_index("pair")
    occ_dev = half_ints.shape[0]
    pair_dev = pno_coef.shape[1]
    fit_width = half_ints.shape[2]
    pno_width = pno_coef.shape[3]
    part_count = partners.shape[1]
    group_size = pair_count * pair_dev
    local_orbital = pair_list[:, :, 0] - my_pair * occ_dev
    candidates = jnp.einsum(
        "obf,cpba->cpofa", half_ints, pno_coef, preferred_element_type=jnp.float32
    )
    orbital_iota = lax.broadcasted_iota(jnp.int32, (1, 1, occ_dev), 2)
    selector = (local_orbital[:, :, None] == orbital_iota).astype(jnp.float32)
    factor = lax.psum_scatter(
        jnp.sum(selector[:, :, :, None, None] * candidates, axis=2),
        "basis",
        scatter_dimension=0,
        tiled=True,
    )[0].astype(jnp.bfloat16)
    my_list = pick_rows(pair_list, my_basis)
    my_orbital = my_list[:, 0] - my_pair * occ_dev
    domain_flat = fit_domain.reshape(-1)
    domain_rows = take_inside(domain_flat, lax.all_gather(fit_factor, "pair", axis=0, tiled=True))
    row_table = domain_rows.astype(jnp.bfloat16).reshape(occ_dev, fit_width, fit_width)
    chosen = row_table[my_orbital]
    fitted = jnp.einsum("pqr,pqa->pra", chosen, factor, preferred_element_type=jnp.float32).astype(
        jnp.bfloat16
    )
    exchange = (
        jnp.einsum("pra,prb->pab", fitted, fitted, preferred_element_type=jnp.float32) / fit_width
    )
    slot_count = pair_dev * part_count
    flat_partners = partners.reshape(slot_count) - my_basis * group_size
    capacity = max(2, 2 * slot_count // pair_count)
    source = flat_partners // pair_dev
    within = flat_partners % pair_dev
    column_index = lax.broadcasted_iota(jnp.int32, (slot_count, slot_count), 1)
    earlier = column_index < lax.broadcasted_iota(jnp.int32, (slot_count, slot_count), 0)
    slot_rank = jnp.sum(((source[:, None] == source[None, :]) & earlier).astype(jnp.int32), axis=1)
    position = source * capacity + slot_rank
    places = lax.broadcasted_iota(jnp.int32, (pair_count * capacity, slot_count), 0)
    wanted = jnp.sum(jnp.where(places == position[None, :], within[None, :], 0), axis=1)
    wanted = wanted.reshape(pair_count, capacity)
    outgoing = amplitudes[lax.all_to_all(wanted, "pair", split_axis=0, concat_axis=0, tiled=True)]
    arrived = lax.all_to_all(outgoing, "pair", split_axis=0, concat_axis=0, tiled=True)
    picked = arrived.reshape(pair_count * capacity, pno_width, pno_width)[position]
    picked = picked.reshape(pair_dev, part_count, pno_width, pno_width)
    projected = jnp.einsum(
        "psab,psbc->psac", intersections, picked, preferred_element_type=jnp.float32
    ).astype(jnp.bfloat16)
    carried = jnp.einsum(
        "psac,psdc->psad", projected, intersections, preferred_element_type=jnp.float32
    )
    weights = partner_mask.astype(jnp.float32) * coupling
    coupled = jnp.sum(weights[:, :, None, None] * carried, axis=1)
    occ_total = occ_energy.shape[0]
    occ_index = lax.broadcasted_iota(jnp.int32, (1, occ_total), 1)
    first_hit = (my_list[:, 0:1] == occ_index).astype(jnp.float32)
    second_hit = (my_list[:, 1:2] == occ_index).astype(jnp.float32)
    occ_first = jnp.sum(first_hit * occ_energy[None, :], axis=1)
    occ_second = jnp.sum(second_hit * occ_energy[None, :], axis=1)
    occ_sum = occ_first + occ_second
    denominator = pno_energy[:, :, None] + pno_energy[:, None, :] - occ_sum[:, None, None]
    amps = amplitudes.astype(jnp.float32)
    residual = exchange + denominator * amps + coupled
    updated = (amps - residual / denominator).astype(jnp.bfloat16)
    return (residual, updated)


def solution(mesh):
    return jax.shard_map(
        shards,
        mesh=mesh,
        in_specs=(
            P("pair", "basis", None),
            P(None, "pair", "basis", None),
            P(None, "pair", None),
            P("pair", None),
            P("pair", None),
            P(("basis", "pair"), None, None),
            P(("basis", "pair"), None),
            P(),
            P(("basis", "pair"), None),
            P(("basis", "pair"), None),
            P(("basis", "pair"), None, None, None),
            P(("basis", "pair"), None),
        ),
        out_specs=(P(("basis", "pair"), None, None), P(("basis", "pair"), None, None)),
        check_vma=False,
    )
```

profile of v0, /device:TPU:1, one launch (start us, length us, event | category | flops | bytes accessed | tf_op | source)
XLA Modules:
  0.0 130.0 jit_solution(424807815766945787)
XLA Ops:
  8.0 0.0 copy-start
  8.0 0.0 all-gather.2.cloned.1.call-start
  8.1 0.7 all-gather.2.cloned.1.call-update
  8.7 0.0 reduce-scatter.2.cloned.1.call-start
  8.8 0.7 slice_subtract_fusion
  9.5 0.1 fusion.17
  9.6 0.0 copy-start.5
  9.6 0.0 copy-start.1
  9.6 15.1 %multiply_reduce_fusion = f32[4,4,128,256]{3,2,1,0:T(8,128)} fusion(bf16[2,4096,256]{2,1,0:T(8,128)(2,1)} %param.12, bf16[4,4,4096,128]{3,2,1,0:T(8,128)(2,1)} %param.13, f32[4,4,2]{2,1,0:T(4,128)S(1)} %fusion.17), kind=kOutput, calls=%fused_computation.7 | convolution fusion | flops 8591507456 | bytes 23068800 | tf_op jit(solution)/shard_map/obf,cpba->cpofa/dot_general | solution.py:42
  24.7 0.0 reduce-scatter.2.cloned.1.call-update
  24.7 0.0 copy-done.5
  24.7 0.1 sub.73
  24.8 0.2 convert_reduce_fusion
  25.0 0.1 select_reduce_fusion
  25.1 0.1 all_to_all.11
  25.2 15.3 %all_to_all.17 = s32[32,1,2]{2,1,0:T(1,128)S(1)} all-to-all(s32[32,1,2]{2,1,0:T(1,128)S(1)} %bitcast.59), channel_id=1, replica_groups=mesh['basis'=4,'pair'=32] {'pair'}, dimensions={0} | all-to-all | bytes 512 | tf_op jit(solution)/shard_map/all_to_all | solution.py:77
  40.6 0.1 copy.50
  40.7 0.1 copy.51
  40.7 0.1 reshape.247
  40.9 0.0 copy-done.1
  40.9 0.0 copy-start.2
  40.9 0.0 copy-start.6
  40.9 0.0 copy-start.3
  40.9 0.0 copy-start.4
  40.9 2.1 %gather_fusion.2 = bf16[64,128,128]{2,1,0:T(8,128)(2,1)} fusion(bf16[4,128,128]{2,1,0:T(8,128)(2,1)S(1)} %copy-done.1, s32[1024]{0:T(1024)S(1)} %pad_clamp_fusion.1), kind=kCustom, calls=%fused_computation.2 | custom fusion | bytes 4194560 | tf_op jit(solution)/shard_map/gather | solution.py:77
  43.0 4.3 %all-to-all-start.1 = ((bf16[32,2,128,128]{3,2,1,0:T(8,128)(2,1)}), bf16[32,2,128,128]{3,2,1,0:T(8,128)(2,1)S(1)}, u32[]{:S(2)}, u32[]{:S(2)}) async-start(bf16[32,2,128,128]{3,2,1,0:T(8,128)(2,1)} %bitcast.14), calls=%async_computation.2 | async-start | bytes 4194304 | tf_op jit(solution)/shard_map/all_to_all | solution.py:78
  47.4 0.1 sub.75
  47.5 0.0 copy-done.2
  47.5 0.7 dynamic-slice_bitcast_fusion
  48.2 0.0 copy-done.6
  48.2 0.2 select_reduce_fusion.1
  48.5 0.0 copy-done.3
  48.5 0.0 copy-done.4
  48.5 47.8 %all-to-all-done.1 = bf16[32,2,128,128]{3,2,1,0:T(8,128)(2,1)S(1)} async-done(((bf16[32,2,128,128]{3,2,1,0:T(8,128)(2,1)}), bf16[32,2,128,128]{3,2,1,0:T(8,128)(2,1)S(1)}, u32[]{:S(2)}, u32[]{:S(2)}) %all-to-all-start.1) | async-done | bytes 2097184 | tf_op jit(solution)/shard_map/all_to_all | solution.py:78
  96.4 1.7 %gather_fusion.3 = bf16[32,128,128]{2,1,0:T(8,128)(2,1)} fusion(bf16[64,128,128]{2,1,0:T(8,128)(2,1)S(1)} %bitcast.55, s32[1024]{0:T(1024)S(1)} %pad_clamp_fusion), kind=kCustom, calls=%fused_computation.3 | custom fusion | bytes 2097280 | tf_op jit(solution)/shard_map/gather | solution.py:79
  98.0 0.0 copy-start.7
  98.0 0.0 copy-done
  98.0 2.8 %multiply_reduce_fusion.1 = f32[4,128,128]{2,1,0:T(8,128)S(1)} fusion(bf16[4,8,128,128]{3,2,1,0:T(8,128)(2,1)S(1)} %copy-done, bf16[4,8,128,128]{3,2,1,0:T(8,128)(2,1)} %bitcast.57, f32[4,8]{1,0:T(4,128)S(1)} %convert_multiply_fusion.1), kind=kOutput, calls=%fused_computation.8 | convolution fusion | flops 269942784 | bytes 2359424 | tf_op jit(solution)/shard_map/psac,psdc->psad/dot_general | solution.py:84
  100.8 8.8 %all-gather.2.cloned.1.call-done = bf16[32768,256]{1,0:T(8,128)(2,1)} async-done(((bf16[1024,256]{1,0:T(8,128)(2,1)}), bf16[32768,256]{1,0:T(8,128)(2,1)}) %all-gather.2.cloned.1.call-update) | async-done | bytes 16777232 | tf_op jit(solution)/shard_map/all_gather | solution.py:56
  109.6 9.5 %gather_fusion = bf16[512,256]{1,0:T(8,128)(2,1)S(1)} fusion(bf16[32768,256]{1,0:T(8,128)(2,1)} %all-gather.2.cloned.1.call-done, s32[1024]{0:T(1024)S(1)} %pad_clamp_fusion.3), kind=kCustom, calls=%fused_computation | custom fusion | bytes 526336 | tf_op jit(solution)/shard_map/jit(_take)/gather | solution.py:14
  119.1 0.2 select_convert_fusion
  119.3 0.6 gather_fusion.1
  119.9 0.0 reduce-scatter.2.cloned.1.call-done
  119.9 0.0 copy-done.7
  120.0 2.6 %fusion.11 = (bf16[4,128,128]{2,1,0:T(8,128)(2,1)}, f32[4,128,128]{2,1,0:T(8,128)}) fusion(bf16[4,128,128]{2,1,0:T(8,128)(2,1)S(1)} %copy-done.1, f32[4]{0:T(128)S(1)} %add.131, f32[4,128]{1,0:T(4,128)S(1)} %copy-done.7, f32[4,128,128]{2,1,0:T(8,128)S(1)} %multiply_reduce_fusion.1, bf16[4,256,256]{2,1,0:T(8,128)(2,1)S(1)} %gather_fusion.1, ...), kind=kOutput, calls=%fused_computation.18 | convolution fusion | flops 101580800 | bytes 1837072 | tf_op jit(solution)/shard_map/pra,prb->pab/dot_general | solution.py:63
  (16 shorter events, 0.1 us)
Async XLA Ops:
  8.0 90.0 %copy-start = (bf16[4,8,128,128]{3,2,1,0:T(8,128)(2,1)S(1)}, bf16[4,8,128,128]{3,2,1,0:T(8,128)(2,1)}, u32[]{:S(2)}) copy-start(bf16[4,8,128,128]{3,2,1,0:T(8,128)(2,1)} %param.22) | copy-start | bytes 3145732
  8.0 101.6 %all-gather.2.cloned.1.call-start = ((), (), s32[]{:S(2)}) async-start(), calls=%async_computation.3 | async-start | bytes 17301504 | tf_op jit(solution)/shard_map/all_gather | solution.py:56
  8.7 111.2 %reduce-scatter.2.cloned.1.call-start = ((), (), s32[]{:S(2)}) async-start(), calls=%async_computation.4 | async-start | bytes 2621440 | tf_op jit(solution)/shard_map/reduce_scatter | solution.py:47
  9.6 15.1 %copy-start.5 = (s32[4,8]{1,0:T(4,128)S(1)}, s32[4,8]{1,0:T(4,128)}, u32[]{:S(2)}) copy-start(s32[4,8]{1,0:T(4,128)} %param.20) | copy-start | bytes 388
  9.6 31.3 %copy-start.1 = (bf16[4,128,128]{2,1,0:T(8,128)(2,1)S(1)}, bf16[4,128,128]{2,1,0:T(8,128)(2,1)}, u32[]{:S(2)}) copy-start(bf16[4,128,128]{2,1,0:T(8,128)(2,1)} %param.17) | copy-start | bytes 393220
  40.9 6.6 %copy-start.2 = (s32[2,256]{1,0:T(2,128)S(1)}, s32[2,256]{1,0:T(2,128)}, u32[]{:S(2)}) copy-start(s32[2,256]{1,0:T(2,128)} %param.15) | copy-start | bytes 6148
  40.9 7.3 %copy-start.6 = (f32[64]{0:T(128)S(1)}, f32[64]{0:T(128)}, u32[]{:S(2)}) copy-start(f32[64]{0:T(128)} %param.19) | copy-start | bytes 772
  40.9 7.6 %copy-start.3 = (f32[4,8]{1,0:T(4,128)S(1)}, f32[4,8]{1,0:T(4,128)}, u32[]{:S(2)}) copy-start(f32[4,8]{1,0:T(4,128)} %param.23) | copy-start | bytes 388
  40.9 7.6 %copy-start.4 = (s32[4,8]{1,0:T(4,128)S(1)}, s32[4,8]{1,0:T(4,128)}, u32[]{:S(2)}) copy-start(s32[4,8]{1,0:T(4,128)} %param.21) | copy-start | bytes 388
  43.0 53.3 %all-to-all-start.1 = ((bf16[32,2,128,128]{3,2,1,0:T(8,128)(2,1)}), bf16[32,2,128,128]{3,2,1,0:T(8,128)(2,1)S(1)}, u32[]{:S(2)}, u32[]{:S(2)}) async-start(bf16[32,2,128,128]{3,2,1,0:T(8,128)(2,1)} %bitcast.14), calls=%async_computation.2 | async-start | bytes 4194304 | tf_op jit(solution)/shard_map/all_to_all | solution.py:78
  98.0 21.9 %copy-start.7 = (f32[4,128]{1,0:T(4,128)S(1)}, f32[4,128]{1,0:T(4,128)}, u32[]{:S(2)}) copy-start(f32[4,128]{1,0:T(4,128)} %param.18) | copy-start | bytes 6148
Sparse Core Ops, SparseCore 0:
  11.1 98.4 all-gather.1
Sparse Core Ops, SparseCore 1:
  24.8 32.9 reduce-scatter.1
where the time goes:
time: 130 us
  waiting for transfers between devices  57.3 us (44%)
  matrix products  20.5 us (16%)
  between operations  15.7 us (12%)
  blocking collectives  15.3 us (12%)
  local copies, waits for them, and re-layouts  15.2 us (12%)
  starting transfers between devices  4.4 us (3%)
  other arithmetic  1.56 us (1%)
    all_to_all x1, waiting for transfers between devices, shards(): lax.all_to_all(outgoing, 'pair', split_axis=0, concat_axis=0, tiled=True)  47.8 us
    all_to_all x1, blocking collectives, shards(): lax.all_to_all(wanted, 'pair', split_axis=0, concat_axis=0, tiled=True)  15.3 us
    dot_general x1, matrix products, shards(): jnp.einsum('obf,cpba->cpofa', half_ints, pno_coef, preferred_element_type...  15.1 us
    gather x1, local copies, waits for them, and re-layouts, take_inside(): taken = jnp.take(shard_rows, safe_index, axis=0).astype(jnp.float32)  9.49 us
    all_gather x1, waiting for transfers between devices, shards(): lax.all_gather(fit_factor, 'pair', axis=0, tiled=True)  8.79 us
    all_to_all x1, starting transfers between devices, shards(): lax.all_to_all(outgoing, 'pair', split_axis=0, concat_axis=0, tiled=True)  4.32 us
    dot_general x1, matrix products, shards(): jnp.einsum('psac,psdc->psad', projected, intersections, preferred_element...  2.79 us
  transfers between devices with their start and end apart: 3, of which 2 were waited for; matrix products, arithmetic and copies ran while one was open for 27% of the time, Pallas kernels for 0%

commit v1 on v0

v1 whole, which is shorter than its diff:
```python
import jax
import jax.numpy as jnp
from jax import lax
from jax.experimental import pallas as pl
from jax.experimental.pallas import tpu as pltpu
from jax.sharding import PartitionSpec as P

BF = jnp.bfloat16
F32 = jnp.float32
MESH = pl.DeviceIdType.MESH
COPIES = 55
VMEM_LIMIT = 60 * 1024 * 1024


def kernel(
    half_hbm, coef_hbm, list_hbm, dom_hbm, fit_hbm, amp_hbm, pen_hbm, occ_hbm,
    part_hbm, mask_hbm, inter_hbm, coup_hbm,
    sum_ref, den_ref,
    hbuf, ht, cb0, cb1, cb2, cb3,
    am, fb, ft, tb, fd, rb, rr, dt, pb, gr2, gr, own, inter, pen,
    list_s, occ_s, part_s, mask_s, coup_s,
    send_sem, recv_sem, h_sem, c_sem, in_sem,
):
    cbs = (cb0, cb1, cb2, cb3)
    z = lax.axis_index("basis")
    pair = lax.axis_index("pair")
    x, y, c = pair // 8, (pair // 2) % 4, pair % 2
    xp, xm, x2 = (x + 1) % 4, (x + 3) % 4, (x + 2) % 4
    yp, ym, y2 = (y + 1) % 4, (y + 3) % 4, (y + 2) % 4
    zp, zm, z2 = (z + 1) % 4, (z + 3) % 4, (z + 2) % 4

    def dev(zz, xx, yy, cc):
        return (zz, (xx * 4 + yy) * 2 + cc)

    to = {
        "xp": dev(z, xp, y, c), "xm": dev(z, xm, y, c),
        "yp": dev(z, x, yp, c), "ym": dev(z, x, ym, c), "y2": dev(z, x, y2, c),
        "zp": dev(zp, x, y, c), "zm": dev(zm, x, y, c), "z2": dev(z2, x, y, c),
        "o": dev(z, x, y, 1 - c),
    }
    started = []
    numbers = {}

    def rdma(name, src, dst, where):
        number = numbers.setdefault(name, len(numbers))
        return pltpu.make_async_remote_copy(
            src_ref=src, dst_ref=dst, send_sem=send_sem.at[number], recv_sem=recv_sem.at[number],
            device_id=to[where], device_id_type=MESH,
        )

    def same(name, ref, where):
        return rdma(name, ref, ref, where)

    every = pl.ds(0, 4)
    cp = {
        "a1p": same("a1p", am.at[x, y, c, pl.ds(0, 2)], "xp"),
        "a1m": same("a1m", am.at[x, y, c, pl.ds(0, 2)], "xm"),
        "a1rp": same("a1rp", am.at[xm, y, c, 0], "xp"),
        "a1rm": same("a1rm", am.at[xp, y, c, 1], "xm"),
        "b1p": same("b1p", am.at[x, y, c, pl.ds(2, 2)], "yp"),
        "b1m": same("b1m", am.at[x, y, c, pl.ds(2, 2)], "ym"),
        "b1rp": same("b1rp", am.at[x, ym, c, 2], "yp"),
        "b1rm": same("b1rm", am.at[x, yp, c, 3], "ym"),
        "a2p0": same("a2p0", am.at[every, y, c, 0], "yp"),
        "a2p1": same("a2p1", am.at[every, y, c, 1], "yp"),
        "a2m0": same("a2m0", am.at[every, y, c, 0], "ym"),
        "a2m1": same("a2m1", am.at[every, y, c, 1], "ym"),
        "a2rp": same("a2rp", am.at[every, ym, c, 0], "yp"),
        "a2rm": same("a2rm", am.at[every, yp, c, 1], "ym"),
        "b2p0": same("b2p0", am.at[x, every, c, 2], "xp"),
        "b2p1": same("b2p1", am.at[x, every, c, 3], "xp"),
        "b2m0": same("b2m0", am.at[x, every, c, 2], "xm"),
        "b2m1": same("b2m1", am.at[x, every, c, 3], "xm"),
        "b2rp": same("b2rp", am.at[xm, every, c, 2], "xp"),
        "b2rm": same("b2rm", am.at[xp, every, c, 3], "xm"),
        "fa1": same("fa1", am.at[every, y, c, pl.ds(0, 2)], "o"),
        "fb1": same("fb1", am.at[x, every, c, pl.ds(2, 2)], "o"),
        "fa2m": same("fa2m", am.at[every, ym, c, pl.ds(0, 2)], "o"),
        "fa2p": same("fa2p", am.at[every, yp, c, pl.ds(0, 2)], "o"),
        "fa20": same("fa20", am.at[every, y2, c, 0], "o"),
        "fa21": same("fa21", am.at[every, y2, c, 1], "o"),
        "fb2m": same("fb2m", am.at[xm, every, c, pl.ds(2, 2)], "o"),
        "fb2p": same("fb2p", am.at[xp, every, c, pl.ds(2, 2)], "o"),
        "fb20": same("fb20", am.at[x2, every, c, 2], "o"),
        "fb21": same("fb21", am.at[x2, every, c, 3], "o"),
        "t1p0": rdma("t1p0", tb.at[0, 0, pl.ds(0, 128)], tb.at[0, 1, pl.ds(0, 128)], "xp"),
        "t1p1": rdma("t1p1", tb.at[0, 0, pl.ds(128, 128)], tb.at[0, 1, pl.ds(128, 128)], "xp"),
        "t1m0": rdma("t1m0", tb.at[0, 0, pl.ds(0, 128)], tb.at[0, 2, pl.ds(0, 128)], "xm"),
        "t1m1": rdma("t1m1", tb.at[0, 0, pl.ds(128, 128)], tb.at[0, 2, pl.ds(128, 128)], "xm"),
        "trp": rdma("trp", tb.at[0, 1, pl.ds(0, 128)], tb.at[0, 3, pl.ds(0, 128)], "xp"),
        "trm": rdma("trm", tb.at[0, 2, pl.ds(128, 128)], tb.at[0, 3, pl.ds(128, 128)], "xm"),
        "tf0": rdma("tf0", tb.at[0, 0], tb.at[1, 0], "o"),
        "tf1": rdma("tf1", tb.at[0, 1], tb.at[1, 1], "o"),
        "tf2": rdma("tf2", tb.at[0, 2], tb.at[1, 2], "o"),
        "tf3": rdma("tf3", tb.at[0, 3], tb.at[1, 3], "o"),
        "ip": rdma("ip", fd.at[0], fd.at[1], "yp"),
        "im": rdma("im", fd.at[0], fd.at[2], "ym"),
        "i2": rdma("i2", fd.at[0], fd.at[3], "y2"),
        "rp": rdma("rp", rb.at[2], rr.at[0], "yp"),
        "rm": rdma("rm", rb.at[1], rr.at[1], "ym"),
        "r2": rdma("r2", rb.at[3], rr.at[2], "y2"),
        "zp": rdma("zp", dt.at[pl.ds(0, 2), pl.ds(0, 64)], dt.at[pl.ds(0, 2), pl.ds(64, 64)], "zp"),
        "zm": rdma("zm", dt.at[pl.ds(0, 2), pl.ds(0, 64)], dt.at[pl.ds(0, 2), pl.ds(128, 64)], "zm"),
        "z2": rdma("z2", dt.at[pl.ds(0, 2), pl.ds(0, 64)], dt.at[pl.ds(0, 2), pl.ds(192, 64)], "z2"),
        "g2p": rdma("g2p", pb.at[0, pl.ds(0, 2)], gr2.at[0], "zp"),
        "g2m": rdma("g2m", pb.at[0, pl.ds(2, 2)], gr2.at[1], "zm"),
        "gpa": rdma("gpa", pb.at[1, pl.ds(2, 2)], gr.at[0, pl.ds(2, 2)], "zp"),
        "gpb": rdma("gpb", pb.at[1, pl.ds(0, 2)], gr.at[0, pl.ds(0, 2)], "zp"),
        "gma": rdma("gma", pb.at[2, pl.ds(0, 2)], gr.at[1, pl.ds(0, 2)], "zm"),
        "gmb": rdma("gmb", pb.at[2, pl.ds(2, 2)], gr.at[1, pl.ds(2, 2)], "zm"),
    }

    assert len(numbers) == COPIES

    def go(*names):
        for name in names:
            cp[name].start()
            started.append(name)

    def got(*names):
        for name in names:
            cp[name].wait_recv()

    lane = pl.multiple_of((z // 2) * 128, 128)
    small = [
        pltpu.make_async_copy(amp_hbm, am.at[x, y, c], in_sem.at[0]),
        pltpu.make_async_copy(dom_hbm, fd.at[0], in_sem.at[1]),
        pltpu.make_async_copy(fit_hbm.at[:, pl.ds(lane, 128)], fb, in_sem.at[2]),
        pltpu.make_async_copy(list_hbm, list_s, in_sem.at[3]),
        pltpu.make_async_copy(occ_hbm, occ_s, in_sem.at[4]),
        pltpu.make_async_copy(part_hbm, part_s, in_sem.at[5]),
        pltpu.make_async_copy(mask_hbm, mask_s, in_sem.at[6]),
        pltpu.make_async_copy(coup_hbm, coup_s, in_sem.at[7]),
        pltpu.make_async_copy(pen_hbm, pen, in_sem.at[8]),
    ]
    blocks = [z2, zp, zm, z]

    def h_copy(k, o):
        rows = pl.ds(k * 1024, 1024)
        return pltpu.make_async_copy(half_hbm.at[o, rows], hbuf.at[o, rows], h_sem.at[k * 2 + o])

    def c_copy(k):
        return pltpu.make_async_copy(coef_hbm.at[blocks[k]], cbs[k], c_sem.at[k])

    barrier = pltpu.get_barrier_semaphore()
    for place in to.values():
        pl.semaphore_signal(barrier, inc=1, device_id=place, device_id_type=MESH)
    for copy in small:
        copy.start()
    h_copies = [(h_copy(k, 0), h_copy(k, 1)) for k in range(4)]
    for both in h_copies:
        both[0].start()
        both[1].start()
    c_copies = [c_copy(k) for k in range(4)]
    c_copies[0].start()
    inter_copy = pltpu.make_async_copy(inter_hbm, inter, in_sem.at[9])
    small[0].wait()
    small[1].wait()

    pl.semaphore_wait(barrier, len(to))
    go("a1p", "a1m", "b1p", "b1m", "ip", "im", "i2")
    small[2].wait()
    ft[...] = fb[...].T
    side = pl.multiple_of((z % 2) * 64, 64)
    for h in range(4):
        tb[0, 0, h * 64:(h + 1) * 64, :] = ft[pl.ds(side, 64), h * 256:(h + 1) * 256]
    go("t1p0", "t1m1", "tf0")
    small[3].wait()

    def arrange(block):
        label = [list_s[block, 0, p] & 1 for p in range(4)]
        common = jnp.where(label[0] + label[1] + label[2] + label[3] >= 2, 1, 0)
        like = [1 - (one ^ common) for one in label]
        many = like[0] + like[1] + like[2] + like[3]
        seen = 0
        place = []
        for p in range(4):
            place.append(jnp.where(like[p] == 1, seen, many + p - seen))
            seen = seen + like[p]
        pick = [sum(jnp.where(place[p] == j, p, 0) for p in range(1, 4)) for j in range(4)]
        third = jnp.where(many >= 3, common, 1 - common)
        fourth = jnp.where(many == 4, common, 1 - common)
        return common, pick, third, fourth, place

    plans = [arrange(block) for block in blocks]

    def turn(k):
        for o in range(2):
            for i in range(4):
                part = slice(k * 1024 + i * 256, k * 1024 + (i + 1) * 256)
                ht[o, :, part] = hbuf[o, part, :].T

    def wide(block, i, j):
        pick = plans[block][1]
        return jnp.concatenate([cbs[block][pick[i]], cbs[block][pick[j]]], axis=1)

    def dot(a, b):
        return jnp.dot(a, b, preferred_element_type=F32)

    def halves(out):
        return out[:, :128], out[:, 128:]

    def even(block, other):
        first = dot(ht[plans[block][0]], wide(block, 0, 1))
        second = dot(ht[plans[other][0]], wide(other, 0, 1))
        return halves(first), halves(second)

    def mixed(block):
        weights = wide(block, 2, 3)
        zero = dot(ht[0], weights)
        one = dot(ht[1], weights)
        third, fourth = plans[block][2], plans[block][3]
        return (
            jnp.where(third == 1, one[:, :128], zero[:, :128]),
            jnp.where(fourth == 1, one[:, 128:], zero[:, 128:]),
        )

    def keep(slot, at, pair_of, arrived=None):
        for i in range(2):
            value = pair_of[i]
            if arrived is not None:
                value = value + gr2[arrived, i].astype(F32)
            pb[slot, at + i] = value.astype(BF)

    for k in range(4):
        h_copies[k][0].wait()
        h_copies[k][1].wait()
        turn(k)
        if k == 1:
            c_copies[2].start()
    got("a1p")
    go("a1rp")
    got("a1m")
    go("a1rm")
    got("b1p")
    go("b1rp")
    got("b1m")
    go("b1rm")
    go("t1p1", "t1m0")
    c_copies[0].wait()
    c_copies[1].start()
    keep(0, 2, mixed(0))
    go("g2m")
    got("t1p0")
    go("trp")
    got("t1m1")
    go("trm")
    c_copies[2].wait()
    c_copies[3].start()
    inter_copy.start()
    first, second = even(0, 2)
    keep(0, 0, first)
    go("g2p")
    keep(2, 0, second)
    go("gma")
    got("a1rp", "a1rm")
    go("a2p0", "a2m1", "a2p1", "a2m0", "fa1")
    got("b1rp", "b1rm")
    go("b2p0", "b2m1", "b2p1", "b2m0", "fb1")
    c_copies[1].wait()
    keep(1, 2, mixed(1))
    go("gpa")
    got("t1p1")
    go("tf1")
    got("t1m0")
    go("tf2")
    c_copies[3].wait()
    own[2], own[3] = mixed(3)
    got("trp", "trm")
    go("tf3")
    for i in (4, 5, 6, 7, 8):
        small[i].wait()
    for g in range(4):
        occ = occ_s[list_s[z, 0, g]] + occ_s[list_s[z, 1, g]]
        across = jnp.broadcast_to(pen[g:g + 1, :], (128, 128))
        den_ref[g] = (across.T + across) - occ

    got("tf0", "tf1", "tf2", "tf3", "ip", "im", "i2")
    iota = lax.broadcasted_iota(jnp.int32, (256, 256), 0)
    sources = [
        (k, j, (xx * 4 + y) * 2 + cc)
        for k, cc in ((0, c), (1, 1 - c))
        for j, xx in enumerate((x, xm, xp, x2))
    ]

    def select(j):
        for o in range(2):
            wanted = fd[j, o:o + 1, :]
            owner = wanted >> 10
            row = wanted & 255
            quarter = (wanted >> 8) & 3
            total = jnp.zeros((256, 256), F32)
            for k, i, source in sources:
                key = jnp.where(owner == source, row, -1)
                hot = jnp.where(iota == key, 1.0, 0.0).astype(BF)
                total = total + jnp.dot(tb[k, i], hot, preferred_element_type=F32)
            out = jnp.zeros((64, 256), F32)
            for h in range(4):
                out = out + jnp.where(quarter == h, total[h * 64:(h + 1) * 64], 0.0)
            rb[j, o] = out.astype(BF)

    select(3)
    go("r2")
    select(2)
    go("rp")
    got("b2p0")
    go("b2rp")
    got("b2m1")
    go("b2rm")
    select(1)
    go("rm")
    got("a2p0")
    go("a2rp")
    got("a2m1")
    go("a2rm")
    select(0)
    got("g2p")
    first, second = even(1, 3)
    keep(1, 0, first, 0)
    go("gpb")
    own[0], own[1] = second
    got("g2m")
    keep(2, 2, mixed(2), 1)
    go("gmb")
    got("a2p1")
    go("fa2m")
    got("a2m0")
    go("fa2p")
    got("b2p1")
    go("fb2m")
    got("b2m0")
    go("fb2p")
    got("rp", "rm", "r2")
    for o in range(2):
        dt[o, 0:64, :] = (
            (rb[0, o].astype(F32) + rr[0, o].astype(F32)) + (rr[1, o].astype(F32) + rr[2, o].astype(F32))
        ).astype(BF)
    go("z2", "zp", "zm")
    got("a2rp")
    go("fa20")
    got("a2rm")
    go("fa21")
    got("b2rp")
    go("fb20")
    got("b2rm")
    go("fb21")

    got("gpa", "gpb", "gma", "gmb")
    place = plans[3][4]
    factors = [
        (own[place[g]] + gr[0, place[g]].astype(F32) + gr[1, place[g]].astype(F32)).astype(BF) for g in range(4)
    ]
    inter_copy.wait()
    got("fa1", "fb1", "fa2m", "fa2p", "fa20", "fa21", "fb2m", "fb2p", "fb20", "fb21")
    for g in range(4):
        carried = []
        for s in range(8):
            tile = part_s[g, s] & 127
            picked = am[tile >> 5, (tile >> 3) & 3, (tile >> 2) & 1, tile & 3]
            weight = mask_s[g, s].astype(F32) * coup_s[g, s]
            carried.append((weight * dot(inter[g, s], picked)).astype(BF))
        sum_ref[g] = lax.dot_general(
            jnp.concatenate(carried, axis=1),
            jnp.concatenate([inter[g, s] for s in range(8)], axis=1),
            (((1,), (1,)), ((), ())), preferred_element_type=F32,
        )

    got("zp", "zm", "z2")
    fits = [dot(dt[list_s[z, 0, g] & 1], factors[g]).astype(BF) for g in range(4)]
    for g in range(4):
        exchange = lax.dot_general(fits[g], fits[g], (((0,), (0,)), ((), ())), preferred_element_type=F32)
        sum_ref[g] += exchange / 256
    for name in started:
        cp[name].wait_send()


def shards(
    half_ints, pno_coef, pair_list, fit_domain, fit_factor, amplitudes, pno_energy, occ_energy,
    partners, partner_mask, intersections, coupling,
):
    any_spec = pl.BlockSpec(memory_space=pl.ANY)
    vmem_spec = pl.BlockSpec(memory_space=pltpu.VMEM)
    total, denominator = pl.pallas_call(
        kernel,
        out_shape=(
            jax.ShapeDtypeStruct((4, 128, 128), F32),
            jax.ShapeDtypeStruct((4, 128, 128), F32),
        ),
        in_specs=[any_spec] * 12,
        out_specs=(vmem_spec, vmem_spec),
        scratch_shapes=[
            pltpu.VMEM((2, 4096, 256), BF),
            pltpu.VMEM((2, 256, 4096), BF),
        ]
        + [pltpu.VMEM((4, 4096, 128), BF)] * 4
        + [
            pltpu.VMEM((4, 4, 2, 4, 128, 128), BF),
            pltpu.VMEM((1024, 128), BF),
            pltpu.VMEM((128, 1024), BF),
            pltpu.VMEM((2, 4, 256, 256), BF),
            pltpu.VMEM((4, 2, 256), jnp.int32),
            pltpu.VMEM((4, 2, 64, 256), BF),
            pltpu.VMEM((3, 2, 64, 256), BF),
            pltpu.VMEM((2, 256, 256), BF),
            pltpu.VMEM((3, 4, 256, 128), BF),
            pltpu.VMEM((2, 2, 256, 128), BF),
            pltpu.VMEM((2, 4, 256, 128), BF),
            pltpu.VMEM((4, 256, 128), F32),
            pltpu.VMEM((4, 8, 128, 128), BF),
            pltpu.VMEM((4, 128), F32),
            pltpu.SMEM((4, 2, 4), jnp.int32),
            pltpu.SMEM((64,), F32),
            pltpu.SMEM((4, 8), jnp.int32),
            pltpu.SMEM((4, 8), jnp.int32),
            pltpu.SMEM((4, 8), F32),
            pltpu.SemaphoreType.DMA((COPIES,)),
            pltpu.SemaphoreType.DMA((COPIES,)),
            pltpu.SemaphoreType.DMA((8,)),
            pltpu.SemaphoreType.DMA((4,)),
            pltpu.SemaphoreType.DMA((10,)),
        ],
        compiler_params=pltpu.CompilerParams(
            collective_id=0, has_side_effects=True, vmem_limit_bytes=VMEM_LIMIT
        ),
    )(
        half_ints, pno_coef, jnp.swapaxes(pair_list, 1, 2), fit_domain, fit_factor, amplitudes,
        pno_energy, occ_energy, partners, partner_mask, intersections, coupling,
    )
    amps = amplitudes.astype(F32)
    residual = total + denominator * amps
    return residual, (amps - residual / denominator).astype(BF)


def solution(mesh):
    return jax.shard_map(
        shards,
        mesh=mesh,
        in_specs=(
            P("pair", "basis", None),
            P(None, "pair", "basis", None),
            P(None, "pair", None),
            P("pair", None),
            P("pair", None),
            P(("basis", "pair"), None, None),
            P(("basis", "pair"), None),
            P(),
            P(("basis", "pair"), None),
            P(("basis", "pair"), None),
            P(("basis", "pair"), None, None, None),
            P(("basis", "pair"), None),
        ),
        out_specs=(P(("basis", "pair"), None, None), P(("basis", "pair"), None, None)),
        check_vma=False,
    )
```

time: 130 us -> 37.1 us (0.29)
  waiting for transfers between devices: 57.3 us -> 0 us
  Pallas kernels: 0 us -> 34.5 us
  matrix products: 20.5 us -> 0 us
  blocking collectives: 15.3 us -> 0 us
  local copies, waits for them, and re-layouts: 15.2 us -> 0.01 us
  between operations: 15.7 us -> 0.66 us
  starting transfers between devices: 4.4 us -> 0 us
    all_to_all x1 -> x0, waiting for transfers between devices: 47.8 us -> none  [shards(): lax.all_to_all(outgoing, 'pair', split_axis=0, concat_axis=0, tiled=True)]
    pallas_call x0 -> x1, Pallas kernels: none -> 34.5 us  [shards(): pl.pallas_call(kernel, out_shape=(jax.ShapeDtypeStruct((4, 128, 128), F32...]
    dot_general x3 -> x0, matrix products: 20.5 us -> none  [the longest x1 15.1 us: shards(): jnp.einsum('obf,cpba->cpofa', half_ints, pno_coef, preferred_element_type...]
    all_to_all x1 -> x0, blocking collectives: 15.3 us -> none  [shards(): lax.all_to_all(wanted, 'pair', split_axis=0, concat_axis=0, tiled=True)]
    gather x4 -> x0, local copies, waits for them, and re-layouts: 13.9 us -> none  [the longest x1 9.49 us: take_inside(): taken = jnp.take(shard_rows, safe_index, axis=0).astype(jnp.float32)]
    all_gather x1 -> x0, waiting for transfers between devices: 8.79 us -> none  [shards(): lax.all_gather(fit_factor, 'pair', axis=0, tiled=True)]
    all_to_all x1 -> x0, starting transfers between devices: 4.32 us -> none  [shards(): lax.all_to_all(outgoing, 'pair', split_axis=0, concat_axis=0, tiled=True)]
    convert_element_type x2 -> x1, other arithmetic: 0.28 us -> 1.83 us  [shards(): return (residual, (amps - residual / denominator).astype(BF))]
  transfers between devices with their start and end apart: 3 -> 0, of which waited for: 2 -> 0; matrix products, arithmetic and copies ran while one was open for 27% -> 0% of each run, Pallas kernels for 0% -> 0%
where the time goes in v1:
time: 37.1 us; the launch traced here: 37 us
  Pallas kernels  34.5 us (93%)
  other arithmetic  1.83 us (5%)
  between operations  0.66 us (2%)
    pallas_call x1, Pallas kernels, shards(): pl.pallas_call(kernel, out_shape=(jax.ShapeDtypeStruct((4, 128, 128), F32...  34.5 us
    convert_element_type x1, other arithmetic, shards(): return (residual, (amps - residual / denominator).astype(BF))  1.83 us

profile of v1, /device:TPU:1, one launch (start us, length us, event | category | flops | bytes accessed | tf_op | source)
XLA Modules:
  0.0 37.0 jit_solution(12011493168320881376)
XLA Ops:
  0.6 0.0 copy-start
  0.6 34.5 %shard_map.131 = (f32[4,128,128]{2,1,0:T(8,128)}, f32[4,128,128]{2,1,0:T(8,128)}) custom-call(bf16[2,4096,256]{2,1,0:T(8,128)(2,1)} %half_hbm.1, bf16[4,4,4096,128]{3,2,1,0:T(8,128)(2,1)} %coef_hbm.1, s32[4,2,4]{2,1,0:T(2,128)} %bitcast.1, s32[2,256]{1,0:T(2,128)} %dom_hbm.1, bf16[1024,256]{1,0:T(8,128)(2,1)} %fit_hbm.1, bf16[4,128,128]{2,1,0:T(8,128)(2,1)} %amp_hbm.1, ...), custom_call_target="tpu_custom_call" | custom-call | tf_op jit(solution)/shard_map/pallas_call | solution.py:383
  35.1 0.0 copy-done
  35.1 1.8 %fusion.1 = (bf16[4,128,128]{2,1,0:T(8,128)(2,1)}, f32[4,128,128]{2,1,0:T(8,128)}) fusion(bf16[4,128,128]{2,1,0:T(8,128)(2,1)S(1)} %copy-done, f32[4,128,128]{2,1,0:T(8,128)} %get-tuple-element.5, f32[4,128,128]{2,1,0:T(8,128)} %get-tuple-element.4), kind=kLoop, calls=%fused_computation.3 | loop fusion | flops 393216 | bytes 1048576 | tf_op jit(solution)/shard_map/convert_element_type | solution.py:431
Async XLA Ops:
  0.6 34.5 %copy-start = (bf16[4,128,128]{2,1,0:T(8,128)(2,1)S(1)}, bf16[4,128,128]{2,1,0:T(8,128)(2,1)}, u32[]{:S(2)}) copy-start(bf16[4,128,128]{2,1,0:T(8,128)(2,1)} %amp_hbm.1) | copy-start | bytes 393220

commit v2 on v1

--- a/solution.py
+++ b/solution.py
@@ -8,8 +8,19 @@
 BF = jnp.bfloat16
 F32 = jnp.float32
 MESH = pl.DeviceIdType.MESH
-COPIES = 55
+COPIES = 73
 VMEM_LIMIT = 60 * 1024 * 1024
+
+
+class N:
+    (
+        t1p0, t1m1, b1p, b1m, ip, im, i2, t1p1, t1m0, a1p,
+        a1m, tf0, g2m, trp, trm, b1rp, b1rm, g2p, gma, tf1,
+        tf2, gpa, a1rp, a1rm, b2p0, b2m1, b2p1, b2m0, fb1, tf3,
+        fa1, gmb, gpb, fa2m, fa2p, fb2m, fb2p, fa20, fa21,
+    ) = range(39)
+    a2p, a2m, a2rp, a2rm = range(39, 55, 4)
+    rp, rm, r2, zp, zm, z2, b2rp, b2rm, fb2 = range(55, 73, 2)
 
 
 def kernel(
@@ -39,12 +50,10 @@
         "o": dev(z, x, y, 1 - c),
     }
     started = []
-    numbers = {}
 
     def rdma(name, src, dst, where):
-        number = numbers.setdefault(name, len(numbers))
         return pltpu.make_async_remote_copy(
-            src_ref=src, dst_ref=dst, send_sem=send_sem.at[number], recv_sem=recv_sem.at[number],
+            src_ref=src, dst_ref=dst, send_sem=send_sem.at[name], recv_sem=recv_sem.at[name],
             device_id=to[where], device_id_type=MESH,
         )
 
@@ -53,64 +62,65 @@
 
     every = pl.ds(0, 4)
     cp = {
-        "a1p": same("a1p", am.at[x, y, c, pl.ds(0, 2)], "xp"),
-        "a1m": same("a1m", am.at[x, y, c, pl.ds(0, 2)], "xm"),
-        "a1rp": same("a1rp", am.at[xm, y, c, 0], "xp"),
-        "a1rm": same("a1rm", am.at[xp, y, c, 1], "xm"),
-        "b1p": same("b1p", am.at[x, y, c, pl.ds(2, 2)], "yp"),
-        "b1m": same("b1m", am.at[x, y, c, pl.ds(2, 2)], "ym"),
-        "b1rp": same("b1rp", am.at[x, ym, c, 2], "yp"),
-        "b1rm": same("b1rm", am.at[x, yp, c, 3], "ym"),
-        "a2p0": same("a2p0", am.at[every, y, c, 0], "yp"),
-        "a2p1": same("a2p1", am.at[every, y, c, 1], "yp"),
-        "a2m0": same("a2m0", am.at[every, y, c, 0], "ym"),
-        "a2m1": same("a2m1", am.at[every, y, c, 1], "ym"),
-        "a2rp": same("a2rp", am.at[every, ym, c, 0], "yp"),
-        "a2rm": same("a2rm", am.at[every, yp, c, 1], "ym"),
-        "b2p0": same("b2p0", am.at[x, every, c, 2], "xp"),
-        "b2p1": same("b2p1", am.at[x, every, c, 3], "xp"),
-        "b2m0": same("b2m0", am.at[x, every, c, 2], "xm"),
-        "b2m1": same("b2m1", am.at[x, every, c, 3], "xm"),
-        "b2rp": same("b2rp", am.at[xm, every, c, 2], "xp"),
-        "b2rm": same("b2rm", am.at[xp, every, c, 3], "xm"),
-        "fa1": same("fa1", am.at[every, y, c, pl.ds(0, 2)], "o"),
-        "fb1": same("fb1", am.at[x, every, c, pl.ds(2, 2)], "o"),
-        "fa2m": same("fa2m", am.at[every, ym, c, pl.ds(0, 2)], "o"),
-        "fa2p": same("fa2p", am.at[every, yp, c, pl.ds(0, 2)], "o"),
-        "fa20": same("fa20", am.at[every, y2, c, 0], "o"),
-        "fa21": same("fa21", am.at[every, y2, c, 1], "o"),
-        "fb2m": same("fb2m", am.at[xm, every, c, pl.ds(2, 2)], "o"),
-        "fb2p": same("fb2p", am.at[xp, every, c, pl.ds(2, 2)], "o"),
-        "fb20": same("fb20", am.at[x2, every, c, 2], "o"),
-        "fb21": same("fb21", am.at[x2, every, c, 3], "o"),
-        "t1p0": rdma("t1p0", tb.at[0, 0, pl.ds(0, 128)], tb.at[0, 1, pl.ds(0, 128)], "xp"),
-        "t1p1": rdma("t1p1", tb.at[0, 0, pl.ds(128, 128)], tb.at[0, 1, pl.ds(128, 128)], "xp"),
-        "t1m0": rdma("t1m0", tb.at[0, 0, pl.ds(0, 128)], tb.at[0, 2, pl.ds(0, 128)], "xm"),
-        "t1m1": rdma("t1m1", tb.at[0, 0, pl.ds(128, 128)], tb.at[0, 2, pl.ds(128, 128)], "xm"),
-        "trp": rdma("trp", tb.at[0, 1, pl.ds(0, 128)], tb.at[0, 3, pl.ds(0, 128)], "xp"),
-        "trm": rdma("trm", tb.at[0, 2, pl.ds(128, 128)], tb.at[0, 3, pl.ds(128, 128)], "xm"),
-        "tf0": rdma("tf0", tb.at[0, 0], tb.at[1, 0], "o"),
-        "tf1": rdma("tf1", tb.at[0, 1], tb.at[1, 1], "o"),
-        "tf2": rdma("tf2", tb.at[0, 2], tb.at[1, 2], "o"),
-        "tf3": rdma("tf3", tb.at[0, 3], tb.at[1, 3], "o"),
-        "ip": rdma("ip", fd.at[0], fd.at[1], "yp"),
-        "im": rdma("im", fd.at[0], fd.at[2], "ym"),
-        "i2": rdma("i2", fd.at[0], fd.at[3], "y2"),
-        "rp": rdma("rp", rb.at[2], rr.at[0], "yp"),
-        "rm": rdma("rm", rb.at[1], rr.at[1], "ym"),
-        "r2": rdma("r2", rb.at[3], rr.at[2], "y2"),
-        "zp": rdma("zp", dt.at[pl.ds(0, 2), pl.ds(0, 64)], dt.at[pl.ds(0, 2), pl.ds(64, 64)], "zp"),
-        "zm": rdma("zm", dt.at[pl.ds(0, 2), pl.ds(0, 64)], dt.at[pl.ds(0, 2), pl.ds(128, 64)], "zm"),
-        "z2": rdma("z2", dt.at[pl.ds(0, 2), pl.ds(0, 64)], dt.at[pl.ds(0, 2), pl.ds(192, 64)], "z2"),
-        "g2p": rdma("g2p", pb.at[0, pl.ds(0, 2)], gr2.at[0], "zp"),
-        "g2m": rdma("g2m", pb.at[0, pl.ds(2, 2)], gr2.at[1], "zm"),
-        "gpa": rdma("gpa", pb.at[1, pl.ds(2, 2)], gr.at[0, pl.ds(2, 2)], "zp"),
-        "gpb": rdma("gpb", pb.at[1, pl.ds(0, 2)], gr.at[0, pl.ds(0, 2)], "zp"),
-        "gma": rdma("gma", pb.at[2, pl.ds(0, 2)], gr.at[1, pl.ds(0, 2)], "zm"),
-        "gmb": rdma("gmb", pb.at[2, pl.ds(2, 2)], gr.at[1, pl.ds(2, 2)], "zm"),
+        N.a1p: same(N.a1p, am.at[x, y, c, pl.ds(0, 2)], "xp"),
+        N.a1m: same(N.a1m, am.at[x, y, c, pl.ds(0, 2)], "xm"),
+        N.a1rp: same(N.a1rp, am.at[xm, y, c, 0], "xp"),
+        N.a1rm: same(N.a1rm, am.at[xp, y, c, 1], "xm"),
+        N.b1p: same(N.b1p, am.at[x, y, c, pl.ds(2, 2)], "yp"),
+        N.b1m: same(N.b1m, am.at[x, y, c, pl.ds(2, 2)], "ym"),
+        N.b1rp: same(N.b1rp, am.at[x, ym, c, 2], "yp"),
+        N.b1rm: same(N.b1rm, am.at[x, yp, c, 3], "ym"),
+        N.b2p0: same(N.b2p0, am.at[x, every, c, 2], "xp"),
+        N.b2p1: same(N.b2p1, am.at[x, every, c, 3], "xp"),
+        N.b2m0: same(N.b2m0, am.at[x, every, c, 2], "xm"),
+        N.b2m1: same(N.b2m1, am.at[x, every, c, 3], "xm"),
+        N.fa1: same(N.fa1, am.at[every, y, c, pl.ds(0, 2)], "o"),
+        N.fb1: same(N.fb1, am.at[x, every, c, pl.ds(2, 2)], "o"),
+        N.fa2m: same(N.fa2m, am.at[every, ym, c, pl.ds(0, 2)], "o"),
+        N.fa2p: same(N.fa2p, am.at[every, yp, c, pl.ds(0, 2)], "o"),
+        N.fa20: same(N.fa20, am.at[every, y2, c, 0], "o"),
+        N.fa21: same(N.fa21, am.at[every, y2, c, 1], "o"),
+        N.fb2m: same(N.fb2m, am.at[xm, every, c, pl.ds(2, 2)], "o"),
+        N.fb2p: same(N.fb2p, am.at[xp, every, c, pl.ds(2, 2)], "o"),
+        N.t1p0: rdma(N.t1p0, tb.at[0, 0, pl.ds(0, 128)], tb.at[0, 1, pl.ds(0, 128)], "xp"),
+        N.t1p1: rdma(N.t1p1, tb.at[0, 0, pl.ds(128, 128)], tb.at[0, 1, pl.ds(128, 128)], "xp"),
+        N.t1m0: rdma(N.t1m0, tb.at[0, 0, pl.ds(0, 128)], tb.at[0, 2, pl.ds(0, 128)], "xm"),
+        N.t1m1: rdma(N.t1m1, tb.at[0, 0, pl.ds(128, 128)], tb.at[0, 2, pl.ds(128, 128)], "xm"),
+        N.trp: rdma(N.trp, tb.at[0, 1, pl.ds(0, 128)], tb.at[0, 3, pl.ds(0, 128)], "xp"),
+        N.trm: rdma(N.trm, tb.at[0, 2, pl.ds(128, 128)], tb.at[0, 3, pl.ds(128, 128)], "xm"),
+        N.tf0: rdma(N.tf0, tb.at[0, 0], tb.at[1, 0], "o"),
+        N.tf1: rdma(N.tf1, tb.at[0, 1], tb.at[1, 1], "o"),
+        N.tf2: rdma(N.tf2, tb.at[0, 2], tb.at[1, 2], "o"),
+        N.tf3: rdma(N.tf3, tb.at[0, 3], tb.at[1, 3], "o"),
+        N.ip: rdma(N.ip, fd.at[0], fd.at[1], "yp"),
+        N.im: rdma(N.im, fd.at[0], fd.at[2], "ym"),
+        N.i2: rdma(N.i2, fd.at[0], fd.at[3], "y2"),
+        N.g2p: rdma(N.g2p, pb.at[0, pl.ds(0, 2)], gr2.at[0], "zp"),
+        N.g2m: rdma(N.g2m, pb.at[0, pl.ds(2, 2)], gr2.at[1], "zm"),
+        N.gpa: rdma(N.gpa, pb.at[1, pl.ds(2, 2)], gr.at[0, pl.ds(2, 2)], "zp"),
+        N.gpb: rdma(N.gpb, pb.at[1, pl.ds(0, 2)], gr.at[0, pl.ds(0, 2)], "zp"),
+        N.gma: rdma(N.gma, pb.at[2, pl.ds(0, 2)], gr.at[1, pl.ds(0, 2)], "zm"),
+        N.gmb: rdma(N.gmb, pb.at[2, pl.ds(2, 2)], gr.at[1, pl.ds(2, 2)], "zm"),
     }
 
-    assert len(numbers) == COPIES
+    for j, row in enumerate((x, xm, xp, x2)):
+        cp[N.a2p + j] = same(N.a2p + j, am.at[row, y, c, pl.ds(0, 2)], "yp")
+        cp[N.a2m + j] = same(N.a2m + j, am.at[row, y, c, pl.ds(0, 2)], "ym")
+        cp[N.a2rp + j] = same(N.a2rp + j, am.at[row, ym, c, 0], "yp")
+        cp[N.a2rm + j] = same(N.a2rm + j, am.at[row, yp, c, 1], "ym")
+
+    mine = pl.ds(0, 64)
+    for o in range(2):
+        lines = pl.ds(2 * o, 2)
+        cp[N.b2rp + o] = same(N.b2rp + o, am.at[xm, lines, c, 2], "xp")
+        cp[N.b2rm + o] = same(N.b2rm + o, am.at[xp, lines, c, 3], "xm")
+        cp[N.fb2 + o] = same(N.fb2 + o, am.at[x2, lines, c, pl.ds(2, 2)], "o")
+        cp[N.rp + o] = rdma(N.rp + o, rb.at[2, o], rr.at[0, o], "yp")
+        cp[N.rm + o] = rdma(N.rm + o, rb.at[1, o], rr.at[1, o], "ym")
+        cp[N.r2 + o] = rdma(N.r2 + o, rb.at[3, o], rr.at[2, o], "y2")
+        cp[N.zp + o] = rdma(N.zp + o, dt.at[o, mine], dt.at[o, pl.ds(64, 64)], "zp")
+        cp[N.zm + o] = rdma(N.zm + o, dt.at[o, mine], dt.at[o, pl.ds(128, 64)], "zm")
+        cp[N.z2 + o] = rdma(N.z2 + o, dt.at[o, mine], dt.at[o, pl.ds(192, 64)], "z2")
 
     def go(*names):
         for name in names:
@@ -157,14 +167,13 @@
     small[0].wait()
     small[1].wait()
 
-    pl.semaphore_wait(barrier, len(to))
-    go("a1p", "a1m", "b1p", "b1m", "ip", "im", "i2")
     small[2].wait()
     ft[...] = fb[...].T
     side = pl.multiple_of((z % 2) * 64, 64)
     for h in range(4):
         tb[0, 0, h * 64:(h + 1) * 64, :] = ft[pl.ds(side, 64), h * 256:(h + 1) * 256]
-    go("t1p0", "t1m1", "tf0")
+    pl.semaphore_wait(barrier, len(to))
+    go(N.t1p0, N.t1m1, N.b1p, N.b1m, N.ip, N.im, N.i2, N.t1p1, N.t1m0, N.a1p, N.a1m, N.a2p + 0, N.a2m + 0, N.tf0)
     small[3].wait()
 
     def arrange(block):
@@ -228,130 +237,138 @@
         turn(k)
         if k == 1:
             c_copies[2].start()
-    got("a1p")
-    go("a1rp")
-    got("a1m")
-    go("a1rm")
-    got("b1p")
-    go("b1rp")
-    got("b1m")
-    go("b1rm")
-    go("t1p1", "t1m0")
     c_copies[0].wait()
     c_copies[1].start()
     keep(0, 2, mixed(0))
-    go("g2m")
-    got("t1p0")
-    go("trp")
-    got("t1m1")
-    go("trm")
+    go(N.g2m)
+    got(N.t1p0)
+    go(N.trp)
+    got(N.t1m1)
+    go(N.trm)
+    got(N.b1p)
+    go(N.b1rp)
+    got(N.b1m)
+    go(N.b1rm)
     c_copies[2].wait()
     c_copies[3].start()
     inter_copy.start()
     first, second = even(0, 2)
     keep(0, 0, first)
-    go("g2p")
+    go(N.g2p)
     keep(2, 0, second)
-    go("gma")
-    got("a1rp", "a1rm")
-    go("a2p0", "a2m1", "a2p1", "a2m0", "fa1")
-    got("b1rp", "b1rm")
-    go("b2p0", "b2m1", "b2p1", "b2m0", "fb1")
+    go(N.gma)
+    got(N.a2p + 0)
+    go(N.a2rp + 0)
+    got(N.a2m + 0)
+    go(N.a2rm + 0)
+    got(N.t1p1)
+    go(N.tf1)
+    got(N.t1m0)
+    go(N.tf2)
     c_copies[1].wait()
     keep(1, 2, mixed(1))
-    go("gpa")
-    got("t1p1")
-    go("tf1")
-    got("t1m0")
-    go("tf2")
+    go(N.gpa)
+    got(N.a1p)
+    go(N.a1rp, N.a2p + 1, N.a2m + 1)
+    got(N.a1m)
+    go(N.a1rm, N.a2p + 2, N.a2m + 2)
+    got(N.b1rp, N.b1rm)
+    go(N.b2p0, N.b2m1, N.b2p1, N.b2m0, N.fb1)
+    got(N.trp, N.trm)
+    go(N.tf3)
     c_copies[3].wait()
+    first, second = even(1, 3)
+    own[0], own[1] = second
+    third = mixed(2)
+    got(N.a1rp, N.a1rm)
+    go(N.a2p + 3, N.a2m + 3, N.fa1)
+    got(N.g2m)
+    keep(2, 2, third, 1)
+    go(N.gmb)
+    got(N.g2p)
+    keep(1, 0, first, 0)
+    go(N.gpb)
+
+    got(N.tf0, N.tf1, N.tf2, N.tf3, N.ip, N.im, N.i2)
+    iota = lax.broadcasted_iota(jnp.int32, (256, 256), 0)
+    sources = [
+        (k, j, (xx * 4 + y) * 2 + cc)
+        for k, cc in ((0, c), (1, 1 - c))
+        for j, xx in enumerate((x, xm, xp, x2))
+    ]
+
+    def select(*wanted_of):
+        parts = []
+        for j, o in wanted_of:
+            wanted = fd[j, o:o + 1, :]
+            parts.append((wanted >> 10, wanted & 255, (wanted >> 8) & 3))
+        totals = [jnp.zeros((256, 256), F32) for _ in parts]
+        for k, i, source in sources:
+            for n, (owner, row, _) in enumerate(parts):
+                key = jnp.where(owner == source, row, -1)
+                hot = jnp.where(iota == key, 1.0, 0.0).astype(BF)
+                totals[n] = totals[n] + dot(tb[k, i], hot)
+        for n, (j, o) in enumerate(wanted_of):
+            out = jnp.zeros((64, 256), F32)
+            for h in range(4):
+                out = out + jnp.where(parts[n][2] == h, totals[n][h * 64:(h + 1) * 64], 0.0)
+            rb[j, o] = out.astype(BF)
+
+    def rows(o):
+        got(N.rp + o, N.rm + o, N.r2 + o)
+        dt[o, 0:64, :] = (
+            (rb[0, o].astype(F32) + rr[0, o].astype(F32)) + (rr[1, o].astype(F32) + rr[2, o].astype(F32))
+        ).astype(BF)
+        go(N.z2 + o, N.zp + o, N.zm + o)
+
+    select((3, 0), (2, 0))
+    go(N.r2 + 0, N.rp + 0)
+    select((1, 0), (3, 1))
+    go(N.rm + 0, N.r2 + 1)
+    got(N.b2p0)
+    go(N.b2rp + 0, N.b2rp + 1)
+    got(N.b2m1)
+    go(N.b2rm + 0, N.b2rm + 1)
+    select((2, 1), (1, 1))
+    go(N.rp + 1, N.rm + 1)
+    for j in (1, 2):
+        got(N.a2p + j)
+        go(N.a2rp + j)
+        got(N.a2m + j)
+        go(N.a2rm + j)
+    select((0, 0), (0, 1))
+    got(N.a2p + 3)
+    go(N.a2rp + 3, N.fa2m)
+    got(N.a2m + 3)
+    go(N.a2rm + 3, N.fa2p)
     own[2], own[3] = mixed(3)
-    got("trp", "trm")
-    go("tf3")
+    got(N.b2p1)
+    go(N.fb2m)
+    got(N.b2m0)
+    go(N.fb2p)
+    rows(0)
+    rows(1)
     for i in (4, 5, 6, 7, 8):
         small[i].wait()
     for g in range(4):
         occ = occ_s[list_s[z, 0, g]] + occ_s[list_s[z, 1, g]]
         across = jnp.broadcast_to(pen[g:g + 1, :], (128, 128))
         den_ref[g] = (across.T + across) - occ
-
-    got("tf0", "tf1", "tf2", "tf3", "ip", "im", "i2")
-    iota = lax.broadcasted_iota(jnp.int32, (256, 256), 0)
-    sources = [
-        (k, j, (xx * 4 + y) * 2 + cc)
-        for k, cc in ((0, c), (1, 1 - c))
-        for j, xx in enumerate((x, xm, xp, x2))
-    ]
-
-    def select(j):
-        for o in range(2):
-            wanted = fd[j, o:o + 1, :]
-            owner = wanted >> 10
-            row = wanted & 255
-            quarter = (wanted >> 8) & 3
-            total = jnp.zeros((256, 256), F32)
-            for k, i, source in sources:
-                key = jnp.where(owner == source, row, -1)
-                hot = jnp.where(iota == key, 1.0, 0.0).astype(BF)
-                total = total + jnp.dot(tb[k, i], hot, preferred_element_type=F32)
-            out = jnp.zeros((64, 256), F32)
-            for h in range(4):
-                out = out + jnp.where(quarter == h, total[h * 64:(h + 1) * 64], 0.0)
-            rb[j, o] = out.astype(BF)
-
-    select(3)
-    go("r2")
-    select(2)
-    go("rp")
-    got("b2p0")
-    go("b2rp")
-    got("b2m1")
-    go("b2rm")
-    select(1)
-    go("rm")
-    got("a2p0")
-    go("a2rp")
-    got("a2m1")
-    go("a2rm")
-    select(0)
-    got("g2p")
-    first, second = even(1, 3)
-    keep(1, 0, first, 0)
-    go("gpb")
-    own[0], own[1] = second
-    got("g2m")
-    keep(2, 2, mixed(2), 1)
-    go("gmb")
-    got("a2p1")
-    go("fa2m")
-    got("a2m0")
-    go("fa2p")
-    got("b2p1")
-    go("fb2m")
-    got("b2m0")
-    go("fb2p")
-    got("rp", "rm", "r2")
+    got(N.a2rp + 0, N.a2rp + 1, N.a2rp + 2, N.a2rp + 3)
+    go(N.fa20)
+    got(N.a2rm + 0, N.a2rm + 1, N.a2rm + 2, N.a2rm + 3)
+    go(N.fa21)
     for o in range(2):
-        dt[o, 0:64, :] = (
-            (rb[0, o].astype(F32) + rr[0, o].astype(F32)) + (rr[1, o].astype(F32) + rr[2, o].astype(F32))
-        ).astype(BF)
-    go("z2", "zp", "zm")
-    got("a2rp")
-    go("fa20")
-    got("a2rm")
-    go("fa21")
-    got("b2rp")
-    go("fb20")
-    got("b2rm")
-    go("fb21")
-
-    got("gpa", "gpb", "gma", "gmb")
+        got(N.b2rp + o, N.b2rm + o)
+        go(N.fb2 + o)
+
+    got(N.gpa, N.gpb, N.gma, N.gmb)
     place = plans[3][4]
     factors = [
         (own[place[g]] + gr[0, place[g]].astype(F32) + gr[1, place[g]].astype(F32)).astype(BF) for g in range(4)
     ]
     inter_copy.wait()
-    got("fa1", "fb1", "fa2m", "fa2p", "fa20", "fa21", "fb2m", "fb2p", "fb20", "fb21")
+    got(N.fa1, N.fb1, N.fa2m, N.fa2p, N.fa20, N.fa21, N.fb2m, N.fb2p, N.fb2 + 0, N.fb2 + 1)
     for g in range(4):
         carried = []
         for s in range(8):
@@ -365,7 +382,7 @@
             (((1,), (1,)), ((), ())), preferred_element_type=F32,
         )
 
-    got("zp", "zm", "z2")
+    got(N.zp + 0, N.zm + 0, N.z2 + 0, N.zp + 1, N.zm + 1, N.z2 + 1)
     fits = [dot(dt[list_s[z, 0, g] & 1], factors[g]).astype(BF) for g in range(4)]
     for g in range(4):
         exchange = lax.dot_general(fits[g], fits[g], (((0,), (0,)), ((), ())), preferred_element_type=F32)
@@ -383,8 +400,8 @@
     total, denominator = pl.pallas_call(
         kernel,
         out_shape=(
-            jax.ShapeDtypeStruct((4, 128, 128), F32),
-            jax.ShapeDtypeStruct((4, 128, 128), F32),
+            pltpu.VMEM((4, 128, 128), F32),
+            pltpu.VMEM((4, 128, 128), F32),
         ),
         in_specs=[any_spec] * 12,
         out_specs=(vmem_spec, vmem_spec),

time: 37.1 us -> 32.7 us (0.88)
  Pallas kernels: 34.5 us -> 31.2 us
  other arithmetic: 1.83 us -> 0.8 us
    pallas_call x1, Pallas kernels: 34.5 us -> 31.2 us  [shards(): pl.pallas_call(kernel, out_shape=(pltpu.VMEM((4, 128, 128), F32), pltpu.V...]
    convert_element_type x1, other arithmetic: 1.83 us -> 0.8 us  [shards(): return (residual, (amps - residual / denominator).astype(BF))]
where the time goes in v2:
time: 32.7 us; the launch traced here: 32.6 us
  Pallas kernels  31.2 us (95%)
  other arithmetic  0.8 us (2%)
  between operations  0.66 us (2%)
    pallas_call x1, Pallas kernels, shards(): pl.pallas_call(kernel, out_shape=(pltpu.VMEM((4, 128, 128), F32), pltpu.V...  31.2 us
    convert_element_type x1, other arithmetic, shards(): return (residual, (amps - residual / denominator).astype(BF))  0.8 us

profile of v2, /device:TPU:1, one launch (start us, length us, event | category | flops | bytes accessed | tf_op | source)
XLA Modules:
  0.0 32.6 jit_solution(889301951867035998)
XLA Ops:
  0.6 0.0 copy-start
  0.6 31.2 %shard_map.131 = (f32[4,128,128]{2,1,0:T(8,128)S(1)}, f32[4,128,128]{2,1,0:T(8,128)S(1)}) custom-call(bf16[2,4096,256]{2,1,0:T(8,128)(2,1)} %half_hbm.1, bf16[4,4,4096,128]{3,2,1,0:T(8,128)(2,1)} %coef_hbm.1, s32[4,2,4]{2,1,0:T(2,128)} %bitcast.1, s32[2,256]{1,0:T(2,128)} %dom_hbm.1, bf16[1024,256]{1,0:T(8,128)(2,1)} %fit_hbm.1, ...), custom_call_target="tpu_custom_call" | custom-call | tf_op jit(solution)/shard_map/pallas_call | solution.py:400
  31.8 0.0 copy-done
  31.8 0.8 %fusion.1 = (bf16[4,128,128]{2,1,0:T(8,128)(2,1)}, f32[4,128,128]{2,1,0:T(8,128)}) fusion(bf16[4,128,128]{2,1,0:T(8,128)(2,1)S(1)} %copy-done, f32[4,128,128]{2,1,0:T(8,128)S(1)} %get-tuple-element.5, f32[4,128,128]{2,1,0:T(8,128)S(1)} %get-tuple-element.4), kind=kLoop, calls=%fused_computation.3 | loop fusion | flops 393216 | bytes 1048576 | tf_op jit(solution)/shard_map/convert_element_type | solution.py:448
Async XLA Ops:
  0.6 31.2 %copy-start = (bf16[4,128,128]{2,1,0:T(8,128)(2,1)S(1)}, bf16[4,128,128]{2,1,0:T(8,128)(2,1)}, u32[]{:S(2)}) copy-start(bf16[4,128,128]{2,1,0:T(8,128)(2,1)} %amp_hbm.1) | copy-start | bytes 393220

commit v3 on v2

--- a/solution.py
+++ b/solution.py
@@ -155,8 +155,8 @@
     barrier = pltpu.get_barrier_semaphore()
     for place in to.values():
         pl.semaphore_signal(barrier, inc=1, device_id=place, device_id_type=MESH)
-    for copy in small:
-        copy.start()
+    for i in (2, 0, 1, 3, 4, 5, 6, 7, 8):
+        small[i].start()
     h_copies = [(h_copy(k, 0), h_copy(k, 1)) for k in range(4)]
     for both in h_copies:
         both[0].start()
@@ -164,14 +164,14 @@
     c_copies = [c_copy(k) for k in range(4)]
     c_copies[0].start()
     inter_copy = pltpu.make_async_copy(inter_hbm, inter, in_sem.at[9])
-    small[0].wait()
-    small[1].wait()
 
     small[2].wait()
     ft[...] = fb[...].T
     side = pl.multiple_of((z % 2) * 64, 64)
     for h in range(4):
         tb[0, 0, h * 64:(h + 1) * 64, :] = ft[pl.ds(side, 64), h * 256:(h + 1) * 256]
+    small[0].wait()
+    small[1].wait()
     pl.semaphore_wait(barrier, len(to))
     go(N.t1p0, N.t1m1, N.b1p, N.b1m, N.ip, N.im, N.i2, N.t1p1, N.t1m0, N.a1p, N.a1m, N.a2p + 0, N.a2m + 0, N.tf0)
     small[3].wait()
@@ -368,25 +368,50 @@
         (own[place[g]] + gr[0, place[g]].astype(F32) + gr[1, place[g]].astype(F32)).astype(BF) for g in range(4)
     ]
     inter_copy.wait()
-    got(N.fa1, N.fb1, N.fa2m, N.fa2p, N.fa20, N.fa21, N.fb2m, N.fb2p, N.fb2 + 0, N.fb2 + 1)
-    for g in range(4):
-        carried = []
-        for s in range(8):
-            tile = part_s[g, s] & 127
-            picked = am[tile >> 5, (tile >> 3) & 3, (tile >> 2) & 1, tile & 3]
-            weight = mask_s[g, s].astype(F32) * coup_s[g, s]
-            carried.append((weight * dot(inter[g, s], picked)).astype(BF))
-        sum_ref[g] = lax.dot_general(
-            jnp.concatenate(carried, axis=1),
-            jnp.concatenate([inter[g, s] for s in range(8)], axis=1),
-            (((1,), (1,)), ((), ())), preferred_element_type=F32,
-        )
-
-    got(N.zp + 0, N.zm + 0, N.z2 + 0, N.zp + 1, N.zm + 1, N.z2 + 1)
-    fits = [dot(dt[list_s[z, 0, g] & 1], factors[g]).astype(BF) for g in range(4)]
-    for g in range(4):
-        exchange = lax.dot_general(fits[g], fits[g], (((0,), (0,)), ((), ())), preferred_element_type=F32)
-        sum_ref[g] += exchange / 256
+
+    @pl.when(c == 0)
+    def _():
+        got(N.fa1, N.fb1, N.fa2m, N.fa2p, N.fa20, N.fa21, N.fb2m, N.fb2p, N.fb2 + 0, N.fb2 + 1)
+        for g in range(4):
+            carried = []
+            for s in range(8):
+                tile = part_s[g, s] & 127
+                picked = am[tile >> 5, (tile >> 3) & 3, (tile >> 2) & 1, tile & 3]
+                weight = mask_s[g, s].astype(F32) * coup_s[g, s]
+                carried.append((weight * dot(inter[g, s], picked)).astype(BF))
+            sum_ref[g] = lax.dot_general(
+                jnp.concatenate(carried, axis=1),
+                jnp.concatenate([inter[g, s] for s in range(8)], axis=1),
+                (((1,), (1,)), ((), ())), preferred_element_type=F32,
+            )
+
+        got(N.zp + 0, N.zm + 0, N.z2 + 0, N.zp + 1, N.zm + 1, N.z2 + 1)
+        fits = [dot(dt[list_s[z, 0, g] & 1], factors[g]).astype(BF) for g in range(4)]
+        for g in range(4):
+            exchange = lax.dot_general(fits[g], fits[g], (((0,), (0,)), ((), ())), preferred_element_type=F32)
+            sum_ref[g] += exchange / 256
+
+    @pl.when(c == 1)
+    def _():
+        got(N.zp + 0, N.zm + 0, N.z2 + 0, N.zp + 1, N.zm + 1, N.z2 + 1)
+        fits = [dot(dt[list_s[z, 0, g] & 1], factors[g]).astype(BF) for g in range(4)]
+        for g in range(4):
+            exchange = lax.dot_general(fits[g], fits[g], (((0,), (0,)), ((), ())), preferred_element_type=F32)
+            sum_ref[g] = exchange / 256
+        got(N.fa1, N.fb1, N.fa2m, N.fa2p, N.fa20, N.fa21, N.fb2m, N.fb2p, N.fb2 + 0, N.fb2 + 1)
+        for g in range(4):
+            carried = []
+            for s in range(8):
+                tile = part_s[g, s] & 127
+                picked = am[tile >> 5, (tile >> 3) & 3, (tile >> 2) & 1, tile & 3]
+                weight = mask_s[g, s].astype(F32) * coup_s[g, s]
+                carried.append((weight * dot(inter[g, s], picked)).astype(BF))
+            sum_ref[g] += lax.dot_general(
+                jnp.concatenate(carried, axis=1),
+                jnp.concatenate([inter[g, s] for s in range(8)], axis=1),
+                (((1,), (1,)), ((), ())), preferred_element_type=F32,
+            )
+
     for name in started:
         cp[name].wait_send()
 

time: 32.7 us -> 32.2 us (0.985)
  Pallas kernels: 31.2 us -> 30.7 us
    pallas_call x1, Pallas kernels: 31.2 us -> 30.7 us  [shards(): pl.pallas_call(kernel, out_shape=(pltpu.VMEM((4, 128, 128), F32), pltpu.V...]
where the time goes in v3:
time: 32.2 us; the launch traced here: 32.1 us
  Pallas kernels  30.7 us (95%)
  other arithmetic  0.8 us (2%)
  between operations  0.66 us (2%)
    pallas_call x1, Pallas kernels, shards(): pl.pallas_call(kernel, out_shape=(pltpu.VMEM((4, 128, 128), F32), pltpu.V...  30.7 us
    convert_element_type x1, other arithmetic, shards(): return (residual, (amps - residual / denominator).astype(BF))  0.8 us

profile of v3, /device:TPU:1, one launch (start us, length us, event | category | flops | bytes accessed | tf_op | source)
XLA Modules:
  0.0 32.1 jit_solution(17413081378919400847)
XLA Ops:
  0.6 0.0 copy-start
  0.6 30.7 %shard_map.131 = (f32[4,128,128]{2,1,0:T(8,128)S(1)}, f32[4,128,128]{2,1,0:T(8,128)S(1)}) custom-call(bf16[2,4096,256]{2,1,0:T(8,128)(2,1)} %half_hbm.1, bf16[4,4,4096,128]{3,2,1,0:T(8,128)(2,1)} %coef_hbm.1, s32[4,2,4]{2,1,0:T(2,128)} %bitcast.1, s32[2,256]{1,0:T(2,128)} %dom_hbm.1, bf16[1024,256]{1,0:T(8,128)(2,1)} %fit_hbm.1, ...), custom_call_target="tpu_custom_call" | custom-call | tf_op jit(solution)/shard_map/pallas_call | solution.py:425
  31.3 0.0 copy-done
  31.3 0.8 %fusion.1 = (bf16[4,128,128]{2,1,0:T(8,128)(2,1)}, f32[4,128,128]{2,1,0:T(8,128)}) fusion(bf16[4,128,128]{2,1,0:T(8,128)(2,1)S(1)} %copy-done, f32[4,128,128]{2,1,0:T(8,128)S(1)} %get-tuple-element.5, f32[4,128,128]{2,1,0:T(8,128)S(1)} %get-tuple-element.4), kind=kLoop, calls=%fused_computation.3 | loop fusion | flops 393216 | bytes 1048576 | tf_op jit(solution)/shard_map/convert_element_type | solution.py:473
Async XLA Ops:
  0.6 30.7 %copy-start = (bf16[4,128,128]{2,1,0:T(8,128)(2,1)S(1)}, bf16[4,128,128]{2,1,0:T(8,128)(2,1)}, u32[]{:S(2)}) copy-start(bf16[4,128,128]{2,1,0:T(8,128)(2,1)} %amp_hbm.1) | copy-start | bytes 393220

commit v4 on v3

--- a/solution.py
+++ b/solution.py
@@ -354,13 +354,13 @@
         occ = occ_s[list_s[z, 0, g]] + occ_s[list_s[z, 1, g]]
         across = jnp.broadcast_to(pen[g:g + 1, :], (128, 128))
         den_ref[g] = (across.T + across) - occ
+    for o in range(2):
+        got(N.b2rp + o, N.b2rm + o)
+        go(N.fb2 + o)
     got(N.a2rp + 0, N.a2rp + 1, N.a2rp + 2, N.a2rp + 3)
     go(N.fa20)
     got(N.a2rm + 0, N.a2rm + 1, N.a2rm + 2, N.a2rm + 3)
     go(N.fa21)
-    for o in range(2):
-        got(N.b2rp + o, N.b2rm + o)
-        go(N.fb2 + o)
 
     got(N.gpa, N.gpb, N.gma, N.gmb)
     place = plans[3][4]

time: 32.2 us -> 32 us (level)
  Pallas kernels: 30.7 us -> 30.3 us
    pallas_call x1, Pallas kernels: 30.7 us -> 30.3 us  [shards(): pl.pallas_call(kernel, out_shape=(pltpu.VMEM((4, 128, 128), F32), pltpu.V...]
where the time goes in v4:
time: 32 us; the launch traced here: 31.8 us
  Pallas kernels  30.3 us (95%)
  other arithmetic  0.8 us (2%)
  between operations  0.66 us (2%)
    pallas_call x1, Pallas kernels, shards(): pl.pallas_call(kernel, out_shape=(pltpu.VMEM((4, 128, 128), F32), pltpu.V...  30.3 us
    convert_element_type x1, other arithmetic, shards(): return (residual, (amps - residual / denominator).astype(BF))  0.8 us

profile of v4, /device:TPU:1, one launch (start us, length us, event | category | flops | bytes accessed | tf_op | source)
XLA Modules:
  0.0 31.8 jit_solution(2185185542666284014)
XLA Ops:
  0.6 0.0 copy-start
  0.6 30.3 %shard_map.131 = (f32[4,128,128]{2,1,0:T(8,128)S(1)}, f32[4,128,128]{2,1,0:T(8,128)S(1)}) custom-call(bf16[2,4096,256]{2,1,0:T(8,128)(2,1)} %half_hbm.1, bf16[4,4,4096,128]{3,2,1,0:T(8,128)(2,1)} %coef_hbm.1, s32[4,2,4]{2,1,0:T(2,128)} %bitcast.1, s32[2,256]{1,0:T(2,128)} %dom_hbm.1, bf16[1024,256]{1,0:T(8,128)(2,1)} %fit_hbm.1, ...), custom_call_target="tpu_custom_call" | custom-call | tf_op jit(solution)/shard_map/pallas_call | solution.py:425
  30.9 0.0 copy-done
  30.9 0.8 %fusion.1 = (bf16[4,128,128]{2,1,0:T(8,128)(2,1)}, f32[4,128,128]{2,1,0:T(8,128)}) fusion(bf16[4,128,128]{2,1,0:T(8,128)(2,1)S(1)} %copy-done, f32[4,128,128]{2,1,0:T(8,128)S(1)} %get-tuple-element.5, f32[4,128,128]{2,1,0:T(8,128)S(1)} %get-tuple-element.4), kind=kLoop, calls=%fused_computation.3 | loop fusion | flops 393216 | bytes 1048576 | tf_op jit(solution)/shard_map/convert_element_type | solution.py:473
Async XLA Ops:
  0.6 30.3 %copy-start = (bf16[4,128,128]{2,1,0:T(8,128)(2,1)S(1)}, bf16[4,128,128]{2,1,0:T(8,128)(2,1)}, u32[]{:S(2)}) copy-start(bf16[4,128,128]{2,1,0:T(8,128)(2,1)} %amp_hbm.1) | copy-start | bytes 393220
